TPU v7x, 32 devices: a whole 2x2x4 slice. The times are simulated.
32 devices in a mesh: pix: 16 (over z, y, x), lat: 2 (over core).
Axes of the slice: x: 2, y: 2, z: 4, core: 2. Of those that a mesh axis runs over, the one named last changes fastest.
Arguments:
- latents: bfloat16 [8192, 512], P('pix'), may hold values from -6 to 6
- w_send: bfloat16 [512, 512], P(None, 'lat'), may hold values from -0.25 to 0.25
- w_recv: bfloat16 [512, 512], P(None, 'lat'), may hold values from -0.25 to 0.25
- edge_bias: float32 [512], P('lat'), may hold values from -3 to 3
- w_msg: bfloat16 [512, 512], P('lat'), may hold values from -0.25 to 0.25
- w_self: bfloat16 [512, 512], P(None, 'lat'), may hold values from -0.25 to 0.25
- w_agg: bfloat16 [512, 512], P(None, 'lat'), may hold values from -0.25 to 0.25
- node_bias: float32 [512], P('lat'), may hold values from -3 to 3
- w_node: bfloat16 [512, 512], P('lat'), may hold values from -0.25 to 0.25
- norm_gain: float32 [512], replicated, may hold values from 0.25 to 1.75
- coarse_ids: int32 [128], P('pix'), may hold values from 0 to 511
- send_list: int32 [16], P('pix'), may hold values from 0 to 3
- recv_tile: int32 [512], P('pix'), may hold values from 0 to 3
- send_tile: int32 [512], P('pix'), may hold values from 0 to 6, as said below
- edge_ends: int32 [512, 2, 128], P('pix'), may hold values from 0 to 127
- edge_mask: int32 [512, 128], P('pix'), may hold values 0 or 1
- cotangent: bfloat16 [8192, 512], P('pix'), may hold values from -6 to 6
Outputs:
- new_latents: bfloat16 [8192, 512], P('pix')
- grad_latents: float32 [8192, 512], P('pix', 'lat')
- grad_w_send: float32 [512, 512], P(None, 'lat')
- grad_w_recv: float32 [512, 512], P(None, 'lat')
- grad_edge_bias: float32 [512], P('lat')
- grad_w_msg: float32 [512, 512], P('lat')
- grad_w_self: float32 [512, 512], P(None, 'lat')
- grad_w_agg: float32 [512, 512], P(None, 'lat')
- grad_node_bias: float32 [512], P('lat')
- grad_w_node: float32 [512, 512], P('lat')
- grad_gain: float32 [512], replicated
Inputs may be any that keep to these rules, and one draw needn't show every extreme that they name: `send_tile`: a block's sender tile, numbered as in the first step: first the device's own tiles, then the 1 lent tiles of the preceding and of the following pixel range, then the 1 tiles of the coarse panel; in each device's own run of 32 blocks, the first names a tile lent by the preceding range and the second one lent by the following range. `coarse_ids`: rows may repeat.
All inputs are finite; a program needn't handle non-finite values. No bound on the sum of `edge_mask` on one device may be relied on, other than what follows from the above.
Results may differ from a plain program's by a relative error of at most 0.0085.
Values may be sent and summed in bfloat16 or wider, within the bound.
A program may use at most 128 MiB of HBM per device.

v0:
```python
import math
import jax
import jax.numpy as jnp
from jax import lax
from jax.sharding import PartitionSpec as P

norm_eps = 1e-05


def from_behind(block, axis, distance):
    devices = range(lax.axis_size(axis))
    route = [((i - distance) % len(devices), i) for i in devices]
    return lax.ppermute(block, axis, route)


def silu_slope(values):
    sigma = jax.nn.sigmoid(values)
    return sigma * (1.0 + values * (1.0 - sigma))


def tile_sums(values, offsets, weights, block_tiles, tile_count):
    block_count, tile_len = offsets.shape
    width = values.shape[-1]
    positions = jnp.arange(tile_len, dtype=jnp.int32)
    incidence = (offsets[:, :, None] == positions[None, None, :]).astype(jnp.float32) * weights[
        :, :, None
    ]
    per_block = jnp.einsum(
        "ben,beh->bnh",
        incidence,
        values.reshape(block_count, tile_len, width),
        precision=lax.Precision.HIGHEST,
    )
    tile_ids = jnp.arange(tile_count, dtype=jnp.int32)
    selector = (block_tiles[None, :] == tile_ids[:, None]).astype(jnp.float32)
    summed = jnp.einsum("tb,bnh->tnh", selector, per_block, precision=lax.Precision.HIGHEST)
    return summed.reshape(tile_count * tile_len, width)


def shards(
    latents,
    w_send,
    w_recv,
    edge_bias,
    w_msg,
    w_self,
    w_agg,
    node_bias,
    w_node,
    norm_gain,
    coarse_ids,
    send_list,
    recv_tile,
    send_tile,
    edge_ends,
    edge_mask,
    cotangent,
):
    node_dev, latent_width = latents.shape
    tile_len = edge_ends.shape[2]
    tiles_dev = node_dev // tile_len
    halo_rows = send_list.shape[0] * tile_len
    pix_count = lax.axis_size("pix")
    lat_count = lax.axis_size("lat")
    grad_scale = 1.0 / math.sqrt(node_dev * pix_count)
    hidden_part = w_send.shape[1]
    send_proj = jnp.dot(latents, w_send, preferred_element_type=jnp.float32)
    recv_proj = jnp.dot(latents, w_recv, preferred_element_type=jnp.float32)
    lent_rows = latents.reshape(tiles_dev, tile_len, latent_width)[send_list].reshape(
        halo_rows, latent_width
    )
    from_left = from_behind(lent_rows, "pix", 1)
    from_right = from_behind(lent_rows, "pix", -1)
    side_proj = jnp.dot(
        jnp.concatenate([from_left, from_right], axis=0), w_send, preferred_element_type=jnp.float32
    )
    panel_proj = jnp.dot(
        lax.all_gather(latents[coarse_ids], "pix", axis=0, tiled=True),
        w_send,
        preferred_element_type=jnp.float32,
    )
    source_proj = jnp.concatenate([send_proj, side_proj, panel_proj], axis=0)
    source_tiles = source_proj.shape[0] // tile_len
    sender_offs = edge_ends[:, 0, :]
    receiver_offs = edge_ends[:, 1, :]
    senders = (send_tile[:, None] * tile_len + sender_offs).reshape(-1)
    receivers = (recv_tile[:, None] * tile_len + receiver_offs).reshape(-1)
    mask_rows = edge_mask.astype(jnp.float32)
    edge_weight = mask_rows.reshape(-1)
    unit_rows = jnp.ones_like(mask_rows)
    edge_pre = source_proj[senders] + recv_proj[receivers] + edge_bias
    edge_act = jax.nn.silu(edge_pre).astype(jnp.bfloat16)
    message = jnp.dot(edge_act, w_msg, preferred_element_type=jnp.float32)
    agg_part = tile_sums(message, receiver_offs, mask_rows, recv_tile, tiles_dev)
    aggregate = lax.psum(agg_part, "lat")
    aggregate_bf = aggregate.astype(jnp.bfloat16)
    node_pre = (
        jnp.dot(latents, w_self, preferred_element_type=jnp.float32)
        + jnp.dot(aggregate_bf, w_agg, preferred_element_type=jnp.float32)
        + node_bias
    )
    node_act = jax.nn.silu(node_pre).astype(jnp.bfloat16)
    out_part = jnp.dot(node_act, w_node, preferred_element_type=jnp.float32)
    node_out = lax.psum(out_part, "lat")
    row_mean = jnp.mean(node_out, axis=-1, keepdims=True)
    centered = node_out - row_mean
    row_var = jnp.mean(centered * centered, axis=-1, keepdims=True)
    inv_std = lax.rsqrt(row_var + norm_eps)
    normed = centered * inv_std
    new_latents = (latents.astype(jnp.float32) + normed * norm_gain).astype(jnp.bfloat16)
    grad_out = cotangent.astype(jnp.float32)
    gain_sum = jnp.sum(grad_out * normed, axis=0)
    d_normed = grad_out * norm_gain
    out_cot = inv_std * (
        d_normed
        - jnp.mean(d_normed, axis=-1, keepdims=True)
        - normed * jnp.mean(d_normed * normed, axis=-1, keepdims=True)
    )
    out_cot_bf = out_cot.astype(jnp.bfloat16)
    node_w_grad = jnp.dot(node_act.T, out_cot_bf, preferred_element_type=jnp.float32)
    node_pre_cot = jnp.dot(out_cot_bf, w_node.T, preferred_element_type=jnp.float32) * silu_slope(
        node_pre
    )
    node_bias_sum = jnp.sum(node_pre_cot, axis=0)
    node_pre_bf = node_pre_cot.astype(jnp.bfloat16)
    self_w_grad = jnp.dot(latents.T, node_pre_bf, preferred_element_type=jnp.float32)
    agg_w_grad = jnp.dot(aggregate_bf.T, node_pre_bf, preferred_element_type=jnp.float32)
    latent_part = jnp.dot(node_pre_bf, w_self.T, preferred_element_type=jnp.float32)
    agg_cot_part = jnp.dot(node_pre_bf, w_agg.T, preferred_element_type=jnp.float32)
    agg_cot = lax.psum(agg_cot_part, "lat")
    agg_cot_bf = agg_cot.astype(jnp.bfloat16)
    msg_cot = agg_cot_bf[receivers] * edge_weight.astype(jnp.bfloat16)[:, None]
    msg_w_grad = jnp.dot(edge_act.T, msg_cot, preferred_element_type=jnp.float32)
    pre_cot = jnp.dot(msg_cot, w_msg.T, preferred_element_type=jnp.float32) * silu_slope(edge_pre)
    edge_bias_sum = jnp.sum(pre_cot, axis=0)
    src_cot = tile_sums(pre_cot, sender_offs, unit_rows, send_tile, source_tiles)
    dst_cot = tile_sums(pre_cot, receiver_offs, unit_rows, recv_tile, tiles_dev)
    own_grad = src_cot[:node_dev]
    left_back = src_cot[node_dev : node_dev + halo_rows]
    right_back = src_cot[node_dev + halo_rows : node_dev + 2 * halo_rows]
    panel_part = src_cot[node_dev + 2 * halo_rows :]
    to_left_owner = from_behind(left_back.astype(jnp.bfloat16), "pix", -1).astype(left_back.dtype)
    to_right_owner = from_behind(right_back.astype(jnp.bfloat16), "pix", 1).astype(right_back.dtype)
    returned = (to_left_owner + to_right_owner).reshape(send_list.shape[0], tile_len, hidden_part)
    own_grad = own_grad.reshape(tiles_dev, tile_len, hidden_part).at[send_list].add(returned)
    own_grad = own_grad.reshape(node_dev, hidden_part)
    coarse_grad = lax.psum_scatter(panel_part, "pix", scatter_dimension=0, tiled=True)
    own_grad = own_grad.at[coarse_ids].add(coarse_grad)
    src_cot_bf = own_grad.astype(jnp.bfloat16)
    dst_cot_bf = dst_cot.astype(jnp.bfloat16)
    send_w_grad = jnp.dot(latents.T, src_cot_bf, preferred_element_type=jnp.float32)
    recv_w_grad = jnp.dot(latents.T, dst_cot_bf, preferred_element_type=jnp.float32)
    latent_part = (
        latent_part
        + jnp.dot(src_cot_bf, w_send.T, preferred_element_type=jnp.float32)
        + jnp.dot(dst_cot_bf, w_recv.T, preferred_element_type=jnp.float32)
    )
    share_width = latent_width // lat_count
    lat_index = lax.axis_index("lat")
    lat_share = lax.psum_scatter(
        latent_part.astype(jnp.bfloat16), "lat", scatter_dimension=1, tiled=True
    ).astype(jnp.float32)
    grad_latents = lat_share + lax.dynamic_slice_in_dim(
        grad_out, lat_index * share_width, share_width, 1
    )
    summed = lax.psum(
        (
            send_w_grad,
            recv_w_grad,
            edge_bias_sum,
            msg_w_grad,
            self_w_grad,
            agg_w_grad,
            node_bias_sum,
            node_w_grad,
            gain_sum,
        ),
        "pix",
    )
    scaled = [grad_scale * entry for entry in summed]
    return (
        new_latents,
        grad_latents,
        scaled[0],
        scaled[1],
        scaled[2],
        scaled[3],
        scaled[4],
        scaled[5],
        scaled[6],
        scaled[7],
        scaled[8],
    )


def solution(mesh):
    return jax.shard_map(
        shards,
        mesh=mesh,
        in_specs=(
            P("pix", None),
            P(None, "lat"),
            P(None, "lat"),
            P("lat"),
            P("lat", None),
            P(None, "lat"),
            P(None, "lat"),
            P("lat"),
            P("lat", None),
            P(),
            P("pix"),
            P("pix"),
            P("pix"),
            P("pix"),
            P("pix", None, None),
            P("pix", None),
            P("pix", None),
        ),
        out_specs=(
            P("pix", None),
            P("pix", "lat"),
            P(None, "lat"),
            P(None, "lat"),
            P("lat"),
            P("lat", None),
            P(None, "lat"),
            P(None, "lat"),
            P("lat"),
            P("lat", None),
            P(),
        ),
        check_vma=False,
    )
```

profile of v0, /device:TPU:0, one launch (start us, length us, event | category | flops | bytes accessed | tf_op | source)
XLA Modules:
  0.0 465.5 jit_solution(5024926762899600851)
XLA Ops:
  8.9 3.0 collective-permute-start
  11.9 4.1 collective-permute-start.1
  16.6 1.7 gather_fusion
  18.3 38.1 %all-gather = bf16[128,512]{1,0:T(8,128)(2,1)S(1)} all-gather(bf16[8,512]{1,0:T(8,128)(2,1)S(1)} %gather_fusion), channel_id=2, replica_groups=mesh['pix'=16,'lat'=2] {'pix'}, dimensions={0}, use_global_device_ids=true | all-gather | bytes 139264 | tf_op jit(solution)/shard_map/all_gather | solution.py:78
  56.4 1.4 fusion.52
  57.8 1.1 fusion.53
  62.2 1.4 fusion.54
  63.6 1.2 fusion.51
  64.9 16.1 %gather_fusion.2 = f32[4096,256]{1,0:T(8,128)} fusion(f32[512,256]{1,0:T(8,128)S(1)} %fusion.54, s32[4096]{0:T(1024)S(1)} %broadcast_clamp_fusion), kind=kCustom, calls=%fused_computation.2 | custom fusion | bytes 8404992 | tf_op jit(solution)/shard_map/gather | solution.py:91
  81.3 16.6 %gather_fusion.1 = f32[4096,256]{1,0:T(8,128)} fusion(f32[896,256]{1,0:T(8,128)S(1)} %pad_maximum_fusion, s32[4096]{0:T(1024)S(1)} %broadcast_clamp_fusion.1), kind=kCustom, calls=%fused_computation.1 | custom fusion | bytes 8404992 | tf_op jit(solution)/shard_map/gather | solution.py:91
  97.9 4.9 %multiply_convert_fusion = bf16[4096,256]{1,0:T(8,128)(2,1)S(1)} fusion(f32[256]{0:T(256)S(1)} %copy-done.22, f32[4096,256]{1,0:T(8,128)} %gather_fusion.1, f32[4096,256]{1,0:T(8,128)} %gather_fusion.2), kind=kLoop, calls=%fused_computation.12 | loop fusion | flops 7340032 | bytes 10486784 | tf_op jit(solution)/shard_map/convert_element_type | solution.py:92
  102.9 1.3 fusion.55
  104.2 8.5 %fusion.11 = f32[32,128,512]{2,1,0:T(8,128)S(1)} fusion(f32[32,128,512]{2,1,0:T(8,128)S(1)} %bitcast.85, f32[32,128]{1,0:T(8,128)S(1)} %get-tuple-element.101, s32[32,128]{1,0:T(8,128)S(1)} %bitcast.94), kind=kOutput, calls=%fused_computation.21 | convolution fusion | flops 3222274048 | bytes 16809984 | tf_op jit(solution)/shard_map/ben,beh->bnh/dot_general | solution.py:28
  112.7 7.7 %fusion = f32[4,128,512]{2,0,1:T(4,128)S(1)} fusion(f32[32,128,512]{2,1,0:T(8,128)S(1)} %fusion.11, s32[32]{0:T(128)S(1)} %copy-done.20), kind=kOutput, calls=%fused_computation.5 | convolution fusion | flops 100663424 | bytes 9437312 | tf_op jit(solution)/shard_map/tb,bnh->tnh/dot_general | solution.py:36
  120.8 6.3 %all-reduce.10 = bf16[512,512]{1,0:T(8,128)(2,1)S(1)} all-reduce(f32[512,512]{1,0:T(8,128)S(1)} %bitcast.90), channel_id=1, replica_groups=mesh['pix'=16,'lat'=2] {'lat'}, use_global_device_ids=true, to_apply=%region_0.1 | all-reduce | flops 262144 | bytes 1572864 | tf_op jit(solution)/shard_map/psum | solution.py:95
  127.1 1.3 fusion.16
  129.2 2.2 fusion.45
  132.2 15.1 %all-reduce.7.cloned.1.call-done = f32[512,512]{1,0:T(8,128)} async-done(((f32[512,512]{1,0:T(8,128)}), f32[512,512]{1,0:T(8,128)}) %all-reduce.7.cloned.1.call-update) | async-done | bytes 1048592 | tf_op jit(solution)/shard_map/psum | solution.py:104
  147.3 1.5 reduce_sum.63
  148.8 1.5 multiply_reduce_fusion.2
  150.4 1.8 multiply_reduce_fusion
  152.2 1.3 multiply_convert_fusion.1
  153.8 1.2 fusion.44
  155.3 1.1 fusion.58
  156.5 1.3 fusion.56
  157.8 6.4 %all-reduce.11 = bf16[512,512]{1,0:T(8,128)(2,1)S(1)} all-reduce(f32[512,512]{1,0:T(8,128)S(1)} %fusion.57), channel_id=1, replica_groups=mesh['pix'=16,'lat'=2] {'lat'}, use_global_device_ids=true, to_apply=%region_6.7 | all-reduce | flops 262144 | bytes 1572864 | tf_op jit(solution)/shard_map/psum | solution.py:130
  164.2 17.5 %gather_fusion.3 = bf16[4096,512]{1,0:T(8,128)(2,1)} fusion(bf16[512,512]{1,0:T(8,128)(2,1)S(1)} %all-reduce.11, s32[4096]{0:T(1024)S(1)} %broadcast_clamp_fusion), kind=kCustom, calls=%fused_computation.3 | custom fusion | bytes 8404992 | tf_op jit(solution)/shard_map/gather | solution.py:132
  181.7 5.9 %fusion.50 = (f32[256]{0:T(256)S(1)}, f32[4096,256]{1,0:T(8,128)S(1)}) fusion(f32[256]{0:T(256)S(1)} %copy-done.22, f32[4096,256]{1,0:T(8,128)} %gather_fusion.1, f32[4096,256]{1,0:T(8,128)} %gather_fusion.2, bf16[256,512]{1,0:T(8,128)(2,1)S(1)} %copy-done, bf16[4096,512]{1,0:T(8,128)(2,1)} %gather_fusion.3, bf16[4096]{0:T(1024)(128)(2,1)S(1)} %get-tuple-element.100), kind=kOutput, calls=%fused_computation.107 | convolution fusion | flops 1087373056 | bytes 17049600 | tf_op jit(solution)/shard_map/dot_general | solution.py:134
  187.6 4.4 fusion.13
  192.0 2.7 fusion.14
  194.7 3.8 fusion.49
  198.8 5.5 %collective-permute-start.2 = (bf16[128,256]{1,0:T(8,128)(2,1)S(1)}, bf16[128,256]{1,0:T(8,128)(2,1)S(1)}, u32[]{:S(2)}, u32[]{:S(2)}) collective-permute-start(bf16[128,256]{1,0:T(8,128)(2,1)S(1)} %bitcast.97), channel_id=1, source_target_pairs={{2,0},{4,2},{6,4},{8,6},{10,8},{12,10},{14,12},{16,14},{18,16},{20... | collective-permute-start | bytes 196616 | tf_op jit(solution)/shard_map/ppermute | solution.py:13
  205.5 5.8 %fusion.17 = bf16[4,128,256]{2,0,1:T(4,128)(2,1)S(1)} fusion(f32[32,128,256]{2,1,0:T(8,128)} %fusion.13, s32[32]{0:T(128)S(1)} %copy-done.20), kind=kOutput, calls=%fused_computation.35 | convolution fusion | flops 50462848 | bytes 4456576 | tf_op jit(solution)/shard_map/tb,bnh->tnh/dot_general | solution.py:36
  212.0 1.1 convolution_bitcast_fusion.1
  214.1 1.9 broadcast_select_fusion
  215.9 4.1 scatter-add.12
  220.0 1.1 copy.56
  221.2 61.4 %reduce-scatter.3.cloned.1.call-done = f32[8,256]{1,0:T(8,128)} async-done(((f32[128,256]{1,0:T(8,128)}), f32[8,256]{1,0:T(8,128)}) %reduce-scatter.3.cloned.1.call-update) | async-done | bytes 8208 | tf_op jit(solution)/shard_map/reduce_scatter | solution.py:147
  283.6 1.6 convolution_add_fusion.1
  285.2 2.2 fusion.15
  287.5 2.1 convolution_bitcast_fusion
  289.5 4.5 fusion.6
  294.0 1.1 convolution_bitcast_fusion.2
  295.3 38.9 %all-reduce = (f32[256]{0:T(256)S(1)}, f32[256]{0:T(256)S(1)}, f32[512]{0:T(512)S(1)}) all-reduce(f32[256]{0:T(256)S(1)} %get-tuple-element.105, f32[256]{0:T(256)S(1)} %get-tuple-element.92, f32[512]{0:T(512)S(1)} %get-tuple-element.78), channel_id=1, replica_groups=mesh['pix'=16,'lat'=2] {'pix'}, use_global_device_ids=true, to_apply=%region_14.15 | all-reduce | flops 1024 | bytes 8192 | tf_op jit(solution)/shard_map/psum | solution.py:166
  335.9 1.8 dynamic-slice_add_fusion
  337.8 112.8 %all-reduce.9.cloned.1.call-done = (f32[512,256]{0,1:T(8,128)}, f32[512,256]{0,1:T(8,128)}, f32[256,512]{1,0:T(8,128)}, f32[512,256]{0,1:T(8,128)}, f32[512,256]{0,1:T(8,128)}, /*index=5*/f32[256,512]{1,0:T(8,128)}) async-done(((f32[512,256]{0,1:T(8,128)}, f32[512,256]{0,1:T(8,128)}, f32[256,512]{1,0:T(8,128)}, f32[512,256]{0,1:T(8,128)}, f32[512,256]{0,1:T(8,128)}, /*index=5*/f32[256,512]{1,0:T(8,128)}), ...) | async-done | bytes 3145744 | tf_op jit(solution)/shard_map/psum | solution.py:166
  450.6 1.2 broadcast_multiply_fusion.5
  452.8 1.1 broadcast_multiply_fusion.4
  (108 shorter events, 19.7 us)
Async XLA Ops:
  7.2 95.7 %copy-start = (bf16[256,512]{1,0:T(8,128)(2,1)S(1)}, bf16[256,512]{1,0:T(8,128)(2,1)}, u32[]{:S(2)}) copy-start(bf16[256,512]{1,0:T(8,128)(2,1)} %param.23) | copy-start | bytes 786436
  7.2 56.4 %copy-start.1 = (bf16[512,512]{1,0:T(8,128)(2,1)S(1)}, bf16[512,512]{1,0:T(8,128)(2,1)}, u32[]{:S(2)}) copy-start(bf16[512,512]{1,0:T(8,128)(2,1)} %param.19) | copy-start | bytes 1572868
  7.2 140.1 %all-reduce.7.cloned.1.call-start = ((), (), s32[]{:S(2)}) async-start(), calls=%async_computation.2 | async-start | bytes 2097152 | tf_op jit(solution)/shard_map/psum | solution.py:104
  8.9 72.1 %collective-permute-start = (bf16[128,512]{1,0:T(8,128)(2,1)S(1)}, bf16[128,512]{1,0:T(8,128)(2,1)S(1)}, u32[]{:S(2)}, u32[]{:S(2)}) collective-permute-start(bf16[128,512]{1,0:T(8,128)(2,1)S(1)} %dynamic-slice_bitcast_fusion), channel_id=1, source_target_pairs={{30,0},{0,2},{2,4},{4,6},{6,8},{8,10},{10,12},{12,14},{14,16},{16,... | collective-permute-start | bytes 393224 | tf_op jit(solution)/shard_map/ppermute | solution.py:13
  11.9 69.1 %collective-permute-start.1 = (bf16[128,512]{1,0:T(8,128)(2,1)S(1)}, bf16[128,512]{1,0:T(8,128)(2,1)S(1)}, u32[]{:S(2)}, u32[]{:S(2)}) collective-permute-start(bf16[128,512]{1,0:T(8,128)(2,1)S(1)} %dynamic-slice_bitcast_fusion), channel_id=1, source_target_pairs={{2,0},{4,2},{6,4},{8,6},{10,8},{12,10},{14,12},{16,14},{18,16},{20... | collective-permute-start | bytes 393224 | tf_op jit(solution)/shard_map/ppermute | solution.py:13
  64.9 16.1 %copy-start.18 = (s32[32,128]{1,0:T(8,128)S(1)}, s32[32,128]{1,0:T(8,128)}, u32[]{:S(2)}) copy-start(s32[32,128]{1,0:T(8,128)} %param.34) | copy-start | bytes 49156
  64.9 16.1 %copy-start.8 = (bf16[512,256]{1,0:T(8,128)(2,1)S(1)}, bf16[512,256]{1,0:T(8,128)(2,1)}, u32[]{:S(2)}) copy-start(bf16[512,256]{1,0:T(8,128)(2,1)} %param.20) | copy-start | bytes 786436
  81.3 16.6 %copy-start.22 = (f32[256]{0:T(256)S(1)}, f32[256]{0:T(256)}, u32[]{:S(2)}) copy-start(f32[256]{0:T(256)} %param.22) | copy-start | bytes 3076
  102.8 1.3 copy-start.3
  104.2 8.5 %copy-start.20 = (s32[32]{0:T(128)S(1)}, s32[32]{0:T(128)}, u32[]{:S(2)}) copy-start(s32[32]{0:T(128)} %param.31) | copy-start | bytes 388
  112.7 14.3 %copy-start.21 = (f32[256]{0:T(256)S(1)}, f32[256]{0:T(256)}, u32[]{:S(2)}) copy-start(f32[256]{0:T(256)} %param.26) | copy-start | bytes 3076
  120.4 11.1 %copy-start.24 = (s32[3]{0:T(128)S(1)}, s32[3]{0:T(128)}, u32[]{:S(2)}) copy-start(s32[3]{0:T(128)} %constant.62.clone.1) | copy-start | bytes 40
  127.1 23.3 %copy-start.5 = (bf16[512,512]{1,0:T(8,128)(2,1)S(1)}, bf16[512,512]{1,0:T(8,128)(2,1)}, u32[]{:S(2)}) copy-start(bf16[512,512]{1,0:T(8,128)(2,1)} %param.35) | copy-start | bytes 1572868
  127.1 23.3 %copy-start.19 = (f32[512]{0:T(512)S(1)}, f32[512]{0:T(512)}, u32[]{:S(2)}) copy-start(f32[512]{0:T(512)} %param.28) | copy-start | bytes 6148
  128.4 0.8 copy-start.12
  131.4 22.0 %copy-start.13 = (f32[512,256]{1,0:T(8,128)S(1)}, f32[512,256]{1,0:T(8,128)}, u32[]{:S(2)}) copy-start(f32[512,256]{1,0:T(8,128)} %copy-done.12) | copy-start | bytes 1572868
  131.5 151.1 %reduce-scatter.3.cloned.1.call-start = ((), (), s32[]{:S(2)}) async-start(), calls=%async_computation.3 | async-start | bytes 139264 | tf_op jit(solution)/shard_map/reduce_scatter | solution.py:147
  147.3 4.8 %copy-start.2 = (f32[512,512]{1,0:T(8,128)S(1)}, f32[512,512]{1,0:T(8,128)}, u32[]{:S(2)}) copy-start(f32[512,512]{1,0:T(8,128)} %all-reduce.7.cloned.1.call-done) | copy-start | bytes 3145732
  148.8 4.7 copy-start.25
  153.4 1.6 copy-start.10
  153.4 3.0 copy-start.11
  153.8 2.7 copy-start.7
  192.0 2.7 copy-start.23
  198.8 15.3 %collective-permute-start.2 = (bf16[128,256]{1,0:T(8,128)(2,1)S(1)}, bf16[128,256]{1,0:T(8,128)(2,1)S(1)}, u32[]{:S(2)}, u32[]{:S(2)}) collective-permute-start(bf16[128,256]{1,0:T(8,128)(2,1)S(1)} %bitcast.97), channel_id=1, source_target_pairs={{2,0},{4,2},{6,4},{8,6},{10,8},{12,10},{14,12},{16,14},{18,16},{20... | collective-permute-start | bytes 196616 | tf_op jit(solution)/shard_map/ppermute | solution.py:13
  204.3 9.7 %collective-permute-start.3 = (bf16[128,256]{1,0:T(8,128)(2,1)S(1)}, bf16[128,256]{1,0:T(8,128)(2,1)S(1)}, u32[]{:S(2)}, u32[]{:S(2)}) collective-permute-start(bf16[128,256]{1,0:T(8,128)(2,1)S(1)} %bitcast.98), channel_id=1, source_target_pairs={{30,0},{0,2},{2,4},{4,6},{6,8},{8,10},{10,12},{12,14},{14,16},{16,... | collective-permute-start | bytes 196616 | tf_op jit(solution)/shard_map/ppermute | solution.py:13
  205.2 130.8 %reduce-scatter.5.cloned.1.call-start = ((), (), s32[]{:S(2)}) async-start(), calls=%async_computation.4 | async-start | bytes 786432 | tf_op jit(solution)/shard_map/reduce_scatter | solution.py:160
  211.3 0.7 copy-start.9
  215.9 73.6 %copy-start.4 = (bf16[4096,256]{1,0:T(8,128)(2,1)S(1)}, bf16[4096,256]{1,0:T(8,128)(2,1)}, u32[]{:S(2)}) copy-start(bf16[4096,256]{1,0:T(8,128)(2,1)} %copy-done.3) | copy-start | bytes 6291460
  287.4 163.2 %all-reduce.9.cloned.1.call-start = ((), (), s32[]{:S(2)}) async-start(), calls=%async_computation.5 | async-start | bytes 6291456 | tf_op jit(solution)/shard_map/psum | solution.py:166
  294.0 1.2 copy-start.6
  450.6 4.3 copy-start.17
  450.6 5.4 %copy-start.16 = (f32[512,256]{0,1:T(8,128)S(1)}, f32[512,256]{0,1:T(8,128)}, u32[]{:S(2)}) copy-start(f32[512,256]{0,1:T(8,128)} %get-tuple-element.88) | copy-start | bytes 1572868
  450.6 6.4 %copy-start.15 = (f32[256,512]{1,0:T(8,128)S(1)}, f32[256,512]{1,0:T(8,128)}, u32[]{:S(2)}) copy-start(f32[256,512]{1,0:T(8,128)} %get-tuple-element.89) | copy-start | bytes 1572868
  451.8 6.1 %copy-start.14 = (f32[256,512]{1,0:T(8,128)S(1)}, f32[256,512]{1,0:T(8,128)}, u32[]{:S(2)}) copy-start(f32[256,512]{1,0:T(8,128)} %get-tuple-element.86) | copy-start | bytes 1572868
Sparse Core Ops, SparseCore 0:
  131.6 15.7 all-reduce.6
  205.3 77.1 reduce-scatter.2
  287.5 4.2 reduce-scatter.4
  299.8 150.6 all-reduce.8
where the time goes:
time: 469 us; the launch traced here: 465 us
  waiting for transfers between devices  189 us (40%)
  blocking collectives  89.7 us (19%)
  local copies, waits for them, and re-layouts  67 us (14%)
  matrix products  65.9 us (14%)
  other arithmetic  25.2 us (5%)
  between operations  15.3 us (3%)
  starting transfers between devices  13 us (3%)
    psum x1, waiting for transfers between devices, shards(): lax.psum((send_w_grad, recv_w_grad, edge_bias_sum, msg_w_grad, self_w_gra...  113 us
    reduce_scatter x1, waiting for transfers between devices, shards(): lax.psum_scatter(panel_part, 'pix', scatter_dimension=0, tiled=True)  61.4 us
    psum x1, blocking collectives, shards(): lax.psum((send_w_grad, recv_w_grad, edge_bias_sum, msg_w_grad, self_w_gra...  38.9 us
    all_gather x1, blocking collectives, shards(): lax.all_gather(latents[coarse_ids], 'pix', axis=0, tiled=True)  38.1 us
    gather x2, local copies, waits for them, and re-layouts, shards(): edge_pre = source_proj[senders] + recv_proj[receivers] + edge_bias  32.7 us
    gather x1, local copies, waits for them, and re-layouts, shards(): msg_cot = agg_cot_bf[receivers] * edge_weight.astype(jnp.bfloat16)[:, None]  17.5 us
    dot_general x3, matrix products, tile_sums(): jnp.einsum('tb,bnh->tnh', selector, per_block, precision=lax.Precision.HI...  17.3 us
    dot_general x3, matrix products, tile_sums(): jnp.einsum('ben,beh->bnh', incidence, values.reshape(block_count, tile_le...  15.6 us
  transfers between devices with their start and end apart: 8, of which 3 were waited for; matrix products, arithmetic and copies ran while one was open for 12% of the time, Pallas kernels for 0%

commit v1 on v0

--- a/solution.py
+++ b/solution.py
@@ -5,6 +5,27 @@
 from jax.sharding import PartitionSpec as P
 
 norm_eps = 1e-05
+
+
+def ring_gather(value, axis, dim):
+    size, index, width = (lax.axis_size(axis), lax.axis_index(axis), value.shape[dim])
+    forward = [(i, (i + 1) % size) for i in range(size)]
+    left = [(i, (i - 1) % size) for i in range(size)]
+    out = jnp.zeros((*value.shape[:dim], size * width, *value.shape[dim + 1 :]), value.dtype)
+    out = lax.dynamic_update_slice_in_dim(out, value, index * width, axis=dim)
+    from_left = from_right = value
+    middle = size // 2
+    for lap in range(1, middle + 1):
+        from_left = lax.ppermute(from_left, axis, forward)
+        out = lax.dynamic_update_slice_in_dim(
+            out, from_left, (index - lap) % size * width, axis=dim
+        )
+        if lap < size - middle:
+            from_right = lax.ppermute(from_right, axis, left)
+            out = lax.dynamic_update_slice_in_dim(
+                out, from_right, (index + lap) % size * width, axis=dim
+            )
+    return out
 
 
 def from_behind(block, axis, distance):
@@ -75,9 +96,7 @@
         jnp.concatenate([from_left, from_right], axis=0), w_send, preferred_element_type=jnp.float32
     )
     panel_proj = jnp.dot(
-        lax.all_gather(latents[coarse_ids], "pix", axis=0, tiled=True),
-        w_send,
-        preferred_element_type=jnp.float32,
+        ring_gather(latents[coarse_ids], "pix", 0), w_send, preferred_element_type=jnp.float32
     )
     source_proj = jnp.concatenate([send_proj, side_proj, panel_proj], axis=0)
     source_tiles = source_proj.shape[0] // tile_len

time: 469 us -> 487 us (1.038)
  starting transfers between devices: 13 us -> 52.4 us
  blocking collectives: 89.7 us -> 51.5 us
  waiting for transfers between devices: 189 us -> 206 us
    ppermute x0 -> x15, starting transfers between devices: none -> 40.8 us  [the longest x7 37.8 us: ring_gather(): from_right = lax.ppermute(from_right, axis, left)]
    all_gather x1 -> x0, blocking collectives: 38.1 us -> none  [shards(): lax.all_gather(latents[coarse_ids], 'pix', axis=0, tiled=True)]
    ppermute x0 -> x15, waiting for transfers between devices: none -> 16.9 us  [the longest x8 16.9 us: ring_gather(): from_left = lax.ppermute(from_left, axis, forward)]
  transfers between devices with their start and end apart: 8 -> 23, of which waited for: 3 -> 10; matrix products, arithmetic and copies ran while one was open for 12% -> 11% of each run, Pallas kernels for 0% -> 0%
where the time goes in v1:
time: 487 us; the launch traced here: 482 us
  waiting for transfers between devices  206 us (42%)
  local copies, waits for them, and re-layouts  66.4 us (14%)
  matrix products  64.4 us (13%)
  starting transfers between devices  52.4 us (11%)
  blocking collectives  51.5 us (11%)
  other arithmetic  26 us (5%)
  between operations  15.4 us (3%)
    psum x1, waiting for transfers between devices, shards(): lax.psum((send_w_grad, recv_w_grad, edge_bias_sum, msg_w_grad, self_w_gra...  113 us
    reduce_scatter x1, waiting for transfers between devices, shards(): lax.psum_scatter(panel_part, 'pix', scatter_dimension=0, tiled=True)  61.5 us
    psum x1, blocking collectives, shards(): lax.psum((send_w_grad, recv_w_grad, edge_bias_sum, msg_w_grad, self_w_gra...  38.9 us
    ppermute x7, starting transfers between devices, ring_gather(): from_right = lax.ppermute(from_right, axis, left)  37.8 us
    gather x2, local copies, waits for them, and re-layouts, shards(): edge_pre = source_proj[senders] + recv_proj[receivers] + edge_bias  32.5 us
    gather x1, local copies, waits for them, and re-layouts, shards(): msg_cot = agg_cot_bf[receivers] * edge_weight.astype(jnp.bfloat16)[:, None]  17.8 us
    dot_general x3, matrix products, tile_sums(): jnp.einsum('tb,bnh->tnh', selector, per_block, precision=lax.Precision.HI...  17.3 us
    ppermute x8, waiting for transfers between devices, ring_gather(): from_left = lax.ppermute(from_left, axis, forward)  16.9 us
  transfers between devices with their start and end apart: 23, of which 10 were waited for; matrix products, arithmetic and copies ran while one was open for 11% of the time, Pallas kernels for 0%

profile of v1, /device:TPU:0, one launch (start us, length us, event | category | flops | bytes accessed | tf_op | source)
XLA Modules:
  0.0 482.5 jit_solution(457700939713317495)
XLA Ops:
  7.9 1.7 gather_fusion
  9.6 3.0 collective-permute-start.2
  12.6 4.1 collective-permute-start.3
  18.3 5.6 %collective-permute-start.1 = (bf16[128,512]{1,0:T(8,128)(2,1)S(1)}, bf16[128,512]{1,0:T(8,128)(2,1)S(1)}, u32[]{:S(2)}, u32[]{:S(2)}) collective-permute-start(bf16[128,512]{1,0:T(8,128)(2,1)S(1)} %dynamic-slice_bitcast_fusion), channel_id=1, source_target_pairs={{2,0},{4,2},{6,4},{8,6},{10,8},{12,10},{14,12},{16,14},{18,16},{20... | collective-permute-start | bytes 393224 | tf_op jit(solution)/shard_map/ppermute | solution.py:34
  28.6 1.4 fusion.54
  30.7 1.4 fusion.51
  32.4 16.2 %gather_fusion.2 = f32[4096,256]{1,0:T(8,128)} fusion(f32[512,256]{1,0:T(8,128)S(1)} %fusion.54, s32[4096]{0:T(1024)S(1)} %broadcast_clamp_fusion), kind=kCustom, calls=%fused_computation.2 | custom fusion | bytes 8404992 | tf_op jit(solution)/shard_map/gather | solution.py:110
  48.6 5.6 %collective-permute-start.5 = (bf16[8,512]{1,0:T(8,128)(2,1)S(1)}, bf16[8,512]{1,0:T(8,128)(2,1)S(1)}, u32[]{:S(2)}, u32[]{:S(2)}) collective-permute-start(bf16[8,512]{1,0:T(8,128)(2,1)S(1)} %collective-permute-done.3), channel_id=1, source_target_pairs={{0,30},{2,0},{4,2},{6,4},{8,6},{10,8},{12,10},{14,12},{16,14},{18,... | collective-permute-start | bytes 24584 | tf_op jit(solution)/shard_map/ppermute | solution.py:24
  54.2 1.6 collective-permute-done.4
  55.9 5.6 %collective-permute-start.7 = (bf16[8,512]{1,0:T(8,128)(2,1)S(1)}, bf16[8,512]{1,0:T(8,128)(2,1)S(1)}, u32[]{:S(2)}, u32[]{:S(2)}) collective-permute-start(bf16[8,512]{1,0:T(8,128)(2,1)S(1)} %collective-permute-done.5), channel_id=1, source_target_pairs={{0,30},{2,0},{4,2},{6,4},{8,6},{10,8},{12,10},{14,12},{16,14},{18,... | collective-permute-start | bytes 24584 | tf_op jit(solution)/shard_map/ppermute | solution.py:24
  61.5 1.6 collective-permute-done.6
  63.1 5.6 %collective-permute-start.9 = (bf16[8,512]{1,0:T(8,128)(2,1)S(1)}, bf16[8,512]{1,0:T(8,128)(2,1)S(1)}, u32[]{:S(2)}, u32[]{:S(2)}) collective-permute-start(bf16[8,512]{1,0:T(8,128)(2,1)S(1)} %collective-permute-done.7), channel_id=1, source_target_pairs={{0,30},{2,0},{4,2},{6,4},{8,6},{10,8},{12,10},{14,12},{16,14},{18,... | collective-permute-start | bytes 24584 | tf_op jit(solution)/shard_map/ppermute | solution.py:24
  68.7 1.6 collective-permute-done.8
  70.4 5.6 %collective-permute-start.11 = (bf16[8,512]{1,0:T(8,128)(2,1)S(1)}, bf16[8,512]{1,0:T(8,128)(2,1)S(1)}, u32[]{:S(2)}, u32[]{:S(2)}) collective-permute-start(bf16[8,512]{1,0:T(8,128)(2,1)S(1)} %collective-permute-done.9), channel_id=1, source_target_pairs={{0,30},{2,0},{4,2},{6,4},{8,6},{10,8},{12,10},{14,12},{16,14},{18,... | collective-permute-start | bytes 24584 | tf_op jit(solution)/shard_map/ppermute | solution.py:24
  76.0 1.6 collective-permute-done.10
  77.6 5.6 %collective-permute-start.13 = (bf16[8,512]{1,0:T(8,128)(2,1)S(1)}, bf16[8,512]{1,0:T(8,128)(2,1)S(1)}, u32[]{:S(2)}, u32[]{:S(2)}) collective-permute-start(bf16[8,512]{1,0:T(8,128)(2,1)S(1)} %collective-permute-done.11), channel_id=1, source_target_pairs={{0,30},{2,0},{4,2},{6,4},{8,6},{10,8},{12,10},{14,12},{16,14},{18,... | collective-permute-start | bytes 24584 | tf_op jit(solution)/shard_map/ppermute | solution.py:24
  83.2 1.6 collective-permute-done.12
  84.9 5.6 %collective-permute-start.15 = (bf16[8,512]{1,0:T(8,128)(2,1)S(1)}, bf16[8,512]{1,0:T(8,128)(2,1)S(1)}, u32[]{:S(2)}, u32[]{:S(2)}) collective-permute-start(bf16[8,512]{1,0:T(8,128)(2,1)S(1)} %collective-permute-done.13), channel_id=1, source_target_pairs={{0,30},{2,0},{4,2},{6,4},{8,6},{10,8},{12,10},{14,12},{16,14},{18,... | collective-permute-start | bytes 24584 | tf_op jit(solution)/shard_map/ppermute | solution.py:24
  90.5 1.6 collective-permute-done.14
  92.1 7.2 %collective-permute-done.16 = bf16[8,512]{1,0:T(8,128)(2,1)S(1)} collective-permute-done((bf16[8,512]{1,0:T(8,128)(2,1)S(1)}, bf16[8,512]{1,0:T(8,128)(2,1)S(1)}, u32[]{:S(2)}, u32[]{:S(2)}) %collective-permute-start.16) | collective-permute-done | bytes 8224 | tf_op jit(solution)/shard_map/ppermute | solution.py:19
  99.9 16.3 %gather_fusion.1 = f32[4096,256]{1,0:T(8,128)} fusion(f32[896,256]{1,0:T(8,128)S(1)} %pad_maximum_fusion, s32[4096]{0:T(1024)S(1)} %broadcast_clamp_fusion.1), kind=kCustom, calls=%fused_computation.1 | custom fusion | bytes 8404992 | tf_op jit(solution)/shard_map/gather | solution.py:110
  116.2 4.9 %multiply_convert_fusion = bf16[4096,256]{1,0:T(8,128)(2,1)S(1)} fusion(f32[256]{0:T(256)S(1)} %copy-done.22, f32[4096,256]{1,0:T(8,128)} %gather_fusion.1, f32[4096,256]{1,0:T(8,128)} %gather_fusion.2), kind=kLoop, calls=%fused_computation.12 | loop fusion | flops 7340032 | bytes 10486784 | tf_op jit(solution)/shard_map/convert_element_type | solution.py:111
  122.4 8.5 %fusion.11 = f32[32,128,512]{2,1,0:T(8,128)S(1)} fusion(f32[32,128,512]{2,1,0:T(8,128)S(1)} %bitcast.85, f32[32,128]{1,0:T(8,128)S(1)} %get-tuple-element.101, s32[32,128]{1,0:T(8,128)S(1)} %bitcast.94), kind=kOutput, calls=%fused_computation.21 | convolution fusion | flops 3222274048 | bytes 16809984 | tf_op jit(solution)/shard_map/ben,beh->bnh/dot_general | solution.py:49
  131.0 7.7 %fusion = f32[4,128,512]{2,0,1:T(4,128)S(1)} fusion(f32[32,128,512]{2,1,0:T(8,128)S(1)} %fusion.11, s32[32]{0:T(128)S(1)} %copy-done.20), kind=kOutput, calls=%fused_computation.5 | convolution fusion | flops 100663424 | bytes 9437312 | tf_op jit(solution)/shard_map/tb,bnh->tnh/dot_general | solution.py:57
  139.1 6.3 %all-reduce.10 = bf16[512,512]{1,0:T(8,128)(2,1)S(1)} all-reduce(f32[512,512]{1,0:T(8,128)S(1)} %bitcast.90), channel_id=1, replica_groups=mesh['pix'=16,'lat'=2] {'lat'}, use_global_device_ids=true, to_apply=%region_0.1 | all-reduce | flops 262144 | bytes 1572864 | tf_op jit(solution)/shard_map/psum | solution.py:114
  145.7 2.5 fusion.45
  149.0 15.1 %all-reduce.7.cloned.1.call-done = f32[512,512]{1,0:T(8,128)} async-done(((f32[512,512]{1,0:T(8,128)}), f32[512,512]{1,0:T(8,128)}) %all-reduce.7.cloned.1.call-update) | async-done | bytes 1048592 | tf_op jit(solution)/shard_map/psum | solution.py:123
  164.1 1.5 reduce_sum.63
  165.6 1.5 multiply_reduce_fusion.2
  167.2 1.8 multiply_reduce_fusion
  174.6 6.3 %all-reduce.11 = bf16[512,512]{1,0:T(8,128)(2,1)S(1)} all-reduce(f32[512,512]{1,0:T(8,128)S(1)} %fusion.57), channel_id=1, replica_groups=mesh['pix'=16,'lat'=2] {'lat'}, use_global_device_ids=true, to_apply=%region_6.7 | all-reduce | flops 262144 | bytes 1572864 | tf_op jit(solution)/shard_map/psum | solution.py:149
  181.0 17.8 %gather_fusion.3 = bf16[4096,512]{1,0:T(8,128)(2,1)} fusion(bf16[512,512]{1,0:T(8,128)(2,1)S(1)} %all-reduce.11, s32[4096]{0:T(1024)S(1)} %broadcast_clamp_fusion), kind=kCustom, calls=%fused_computation.3 | custom fusion | bytes 8404992 | tf_op jit(solution)/shard_map/gather | solution.py:151
  198.7 5.9 %fusion.50 = (f32[256]{0:T(256)S(1)}, f32[4096,256]{1,0:T(8,128)S(1)}) fusion(f32[256]{0:T(256)S(1)} %copy-done.22, f32[4096,256]{1,0:T(8,128)} %gather_fusion.1, f32[4096,256]{1,0:T(8,128)} %gather_fusion.2, bf16[256,512]{1,0:T(8,128)(2,1)S(1)} %copy-done, bf16[4096,512]{1,0:T(8,128)(2,1)} %gather_fusion.3, bf16[4096]{0:T(1024)(128)(2,1)S(1)} %get-tuple-element.100), kind=kOutput, calls=%fused_computation.123 | convolution fusion | flops 1087373056 | bytes 17049600 | tf_op jit(solution)/shard_map/dot_general | solution.py:153
  204.7 4.4 fusion.13
  209.1 2.7 fusion.14
  211.7 3.8 fusion.49
  215.8 5.5 %collective-permute-start.17 = (bf16[128,256]{1,0:T(8,128)(2,1)S(1)}, bf16[128,256]{1,0:T(8,128)(2,1)S(1)}, u32[]{:S(2)}, u32[]{:S(2)}) collective-permute-start(bf16[128,256]{1,0:T(8,128)(2,1)S(1)} %bitcast.97), channel_id=1, source_target_pairs={{2,0},{4,2},{6,4},{8,6},{10,8},{12,10},{14,12},{16,14},{18,16},{20... | collective-permute-start | bytes 196616 | tf_op jit(solution)/shard_map/ppermute | solution.py:34
  222.5 5.8 %fusion.17 = bf16[4,128,256]{2,0,1:T(4,128)(2,1)S(1)} fusion(f32[32,128,256]{2,1,0:T(8,128)} %fusion.13, s32[32]{0:T(128)S(1)} %copy-done.20), kind=kOutput, calls=%fused_computation.35 | convolution fusion | flops 50462848 | bytes 4456576 | tf_op jit(solution)/shard_map/tb,bnh->tnh/dot_general | solution.py:57
  231.1 1.9 broadcast_select_fusion
  232.9 4.1 scatter-add.12
  238.1 61.5 %reduce-scatter.3.cloned.1.call-done = f32[8,256]{1,0:T(8,128)} async-done(((f32[128,256]{1,0:T(8,128)}), f32[8,256]{1,0:T(8,128)}) %reduce-scatter.3.cloned.1.call-update) | async-done | bytes 8208 | tf_op jit(solution)/shard_map/reduce_scatter | solution.py:166
  300.7 1.6 convolution_add_fusion.1
  302.3 2.2 fusion.15
  304.5 2.1 convolution_bitcast_fusion
  306.6 4.5 fusion.6
  312.4 38.9 %all-reduce = (f32[256]{0:T(256)S(1)}, f32[256]{0:T(256)S(1)}, f32[512]{0:T(512)S(1)}) all-reduce(f32[256]{0:T(256)S(1)} %get-tuple-element.105, f32[256]{0:T(256)S(1)} %get-tuple-element.92, f32[512]{0:T(512)S(1)} %get-tuple-element.78), channel_id=1, replica_groups=mesh['pix'=16,'lat'=2] {'pix'}, use_global_device_ids=true, to_apply=%region_14.15 | all-reduce | flops 1024 | bytes 8192 | tf_op jit(solution)/shard_map/psum | solution.py:185
  353.0 1.8 dynamic-slice_add_fusion
  354.8 112.8 %all-reduce.9.cloned.1.call-done = (f32[512,256]{0,1:T(8,128)}, f32[512,256]{0,1:T(8,128)}, f32[256,512]{1,0:T(8,128)}, f32[512,256]{0,1:T(8,128)}, f32[512,256]{0,1:T(8,128)}, /*index=5*/f32[256,512]{1,0:T(8,128)}) async-done(((f32[512,256]{0,1:T(8,128)}, f32[512,256]{0,1:T(8,128)}, f32[256,512]{1,0:T(8,128)}, f32[512,256]{0,1:T(8,128)}, f32[512,256]{0,1:T(8,128)}, /*index=5*/f32[256,512]{1,0:T(8,128)}), ...) | async-done | bytes 3145744 | tf_op jit(solution)/shard_map/psum | solution.py:185
  (154 shorter events, 33.4 us)
Async XLA Ops:
  7.2 113.9 %copy-start = (bf16[256,512]{1,0:T(8,128)(2,1)S(1)}, bf16[256,512]{1,0:T(8,128)(2,1)}, u32[]{:S(2)}) copy-start(bf16[256,512]{1,0:T(8,128)(2,1)} %param.23) | copy-start | bytes 786436
  7.2 156.9 %all-reduce.7.cloned.1.call-start = ((), (), s32[]{:S(2)}) async-start(), calls=%async_computation.2 | async-start | bytes 2097152 | tf_op jit(solution)/shard_map/psum | solution.py:123
  9.6 39.0 %collective-permute-start.2 = (bf16[8,512]{1,0:T(8,128)(2,1)S(1)}, bf16[8,512]{1,0:T(8,128)(2,1)S(1)}, u32[]{:S(2)}, u32[]{:S(2)}) collective-permute-start(bf16[8,512]{1,0:T(8,128)(2,1)S(1)} %gather_fusion), channel_id=1, source_target_pairs={{0,2},{2,4},{4,6},{6,8},{8,10},{10,12},{12,14},{14,16},{16,18},{18... | collective-permute-start | bytes 24584 | tf_op jit(solution)/shard_map/ppermute | solution.py:19
  12.6 36.0 %collective-permute-start.3 = (bf16[8,512]{1,0:T(8,128)(2,1)S(1)}, bf16[8,512]{1,0:T(8,128)(2,1)S(1)}, u32[]{:S(2)}, u32[]{:S(2)}) collective-permute-start(bf16[8,512]{1,0:T(8,128)(2,1)S(1)} %gather_fusion), channel_id=1, source_target_pairs={{0,30},{2,0},{4,2},{6,4},{8,6},{10,8},{12,10},{14,12},{16,14},{18,... | collective-permute-start | bytes 24584 | tf_op jit(solution)/shard_map/ppermute | solution.py:24
  18.2 81.3 %collective-permute-start = (bf16[128,512]{1,0:T(8,128)(2,1)S(1)}, bf16[128,512]{1,0:T(8,128)(2,1)S(1)}, u32[]{:S(2)}, u32[]{:S(2)}) collective-permute-start(bf16[128,512]{1,0:T(8,128)(2,1)S(1)} %dynamic-slice_bitcast_fusion), channel_id=1, source_target_pairs={{30,0},{0,2},{2,4},{4,6},{6,8},{8,10},{10,12},{12,14},{14,16},{16,... | collective-permute-start | bytes 393224 | tf_op jit(solution)/shard_map/ppermute | solution.py:34
  18.3 81.3 %collective-permute-start.1 = (bf16[128,512]{1,0:T(8,128)(2,1)S(1)}, bf16[128,512]{1,0:T(8,128)(2,1)S(1)}, u32[]{:S(2)}, u32[]{:S(2)}) collective-permute-start(bf16[128,512]{1,0:T(8,128)(2,1)S(1)} %dynamic-slice_bitcast_fusion), channel_id=1, source_target_pairs={{2,0},{4,2},{6,4},{8,6},{10,8},{12,10},{14,12},{16,14},{18,16},{20... | collective-permute-start | bytes 393224 | tf_op jit(solution)/shard_map/ppermute | solution.py:34
  32.4 67.0 %copy-start.8 = (bf16[512,256]{1,0:T(8,128)(2,1)S(1)}, bf16[512,256]{1,0:T(8,128)(2,1)}, u32[]{:S(2)}) copy-start(bf16[512,256]{1,0:T(8,128)(2,1)} %param.20) | copy-start | bytes 786436
  48.6 7.2 %collective-permute-start.4 = (bf16[8,512]{1,0:T(8,128)(2,1)S(1)}, bf16[8,512]{1,0:T(8,128)(2,1)S(1)}, u32[]{:S(2)}, u32[]{:S(2)}) collective-permute-start(bf16[8,512]{1,0:T(8,128)(2,1)S(1)} %collective-permute-done.2), channel_id=1, source_target_pairs={{0,2},{2,4},{4,6},{6,8},{8,10},{10,12},{12,14},{14,16},{16,18},{18... | collective-permute-start | bytes 24584 | tf_op jit(solution)/shard_map/ppermute | solution.py:19
  48.6 7.2 %collective-permute-start.5 = (bf16[8,512]{1,0:T(8,128)(2,1)S(1)}, bf16[8,512]{1,0:T(8,128)(2,1)S(1)}, u32[]{:S(2)}, u32[]{:S(2)}) collective-permute-start(bf16[8,512]{1,0:T(8,128)(2,1)S(1)} %collective-permute-done.3), channel_id=1, source_target_pairs={{0,30},{2,0},{4,2},{6,4},{8,6},{10,8},{12,10},{14,12},{16,14},{18,... | collective-permute-start | bytes 24584 | tf_op jit(solution)/shard_map/ppermute | solution.py:24
  55.9 7.2 %collective-permute-start.6 = (bf16[8,512]{1,0:T(8,128)(2,1)S(1)}, bf16[8,512]{1,0:T(8,128)(2,1)S(1)}, u32[]{:S(2)}, u32[]{:S(2)}) collective-permute-start(bf16[8,512]{1,0:T(8,128)(2,1)S(1)} %collective-permute-done.4), channel_id=1, source_target_pairs={{0,2},{2,4},{4,6},{6,8},{8,10},{10,12},{12,14},{14,16},{16,18},{18... | collective-permute-start | bytes 24584 | tf_op jit(solution)/shard_map/ppermute | solution.py:19
  55.9 7.2 %collective-permute-start.7 = (bf16[8,512]{1,0:T(8,128)(2,1)S(1)}, bf16[8,512]{1,0:T(8,128)(2,1)S(1)}, u32[]{:S(2)}, u32[]{:S(2)}) collective-permute-start(bf16[8,512]{1,0:T(8,128)(2,1)S(1)} %collective-permute-done.5), channel_id=1, source_target_pairs={{0,30},{2,0},{4,2},{6,4},{8,6},{10,8},{12,10},{14,12},{16,14},{18,... | collective-permute-start | bytes 24584 | tf_op jit(solution)/shard_map/ppermute | solution.py:24
  63.1 7.2 %collective-permute-start.8 = (bf16[8,512]{1,0:T(8,128)(2,1)S(1)}, bf16[8,512]{1,0:T(8,128)(2,1)S(1)}, u32[]{:S(2)}, u32[]{:S(2)}) collective-permute-start(bf16[8,512]{1,0:T(8,128)(2,1)S(1)} %collective-permute-done.6), channel_id=1, source_target_pairs={{0,2},{2,4},{4,6},{6,8},{8,10},{10,12},{12,14},{14,16},{16,18},{18... | collective-permute-start | bytes 24584 | tf_op jit(solution)/shard_map/ppermute | solution.py:19
  63.1 7.2 %collective-permute-start.9 = (bf16[8,512]{1,0:T(8,128)(2,1)S(1)}, bf16[8,512]{1,0:T(8,128)(2,1)S(1)}, u32[]{:S(2)}, u32[]{:S(2)}) collective-permute-start(bf16[8,512]{1,0:T(8,128)(2,1)S(1)} %collective-permute-done.7), channel_id=1, source_target_pairs={{0,30},{2,0},{4,2},{6,4},{8,6},{10,8},{12,10},{14,12},{16,14},{18,... | collective-permute-start | bytes 24584 | tf_op jit(solution)/shard_map/ppermute | solution.py:24
  70.4 7.2 %collective-permute-start.10 = (bf16[8,512]{1,0:T(8,128)(2,1)S(1)}, bf16[8,512]{1,0:T(8,128)(2,1)S(1)}, u32[]{:S(2)}, u32[]{:S(2)}) collective-permute-start(bf16[8,512]{1,0:T(8,128)(2,1)S(1)} %collective-permute-done.8), channel_id=1, source_target_pairs={{0,2},{2,4},{4,6},{6,8},{8,10},{10,12},{12,14},{14,16},{16,18},{18... | collective-permute-start | bytes 24584 | tf_op jit(solution)/shard_map/ppermute | solution.py:19
  70.4 7.2 %collective-permute-start.11 = (bf16[8,512]{1,0:T(8,128)(2,1)S(1)}, bf16[8,512]{1,0:T(8,128)(2,1)S(1)}, u32[]{:S(2)}, u32[]{:S(2)}) collective-permute-start(bf16[8,512]{1,0:T(8,128)(2,1)S(1)} %collective-permute-done.9), channel_id=1, source_target_pairs={{0,30},{2,0},{4,2},{6,4},{8,6},{10,8},{12,10},{14,12},{16,14},{18,... | collective-permute-start | bytes 24584 | tf_op jit(solution)/shard_map/ppermute | solution.py:24
  77.6 7.2 %collective-permute-start.12 = (bf16[8,512]{1,0:T(8,128)(2,1)S(1)}, bf16[8,512]{1,0:T(8,128)(2,1)S(1)}, u32[]{:S(2)}, u32[]{:S(2)}) collective-permute-start(bf16[8,512]{1,0:T(8,128)(2,1)S(1)} %collective-permute-done.10), channel_id=1, source_target_pairs={{0,2},{2,4},{4,6},{6,8},{8,10},{10,12},{12,14},{14,16},{16,18},{18... | collective-permute-start | bytes 24584 | tf_op jit(solution)/shard_map/ppermute | solution.py:19
  77.6 7.2 %collective-permute-start.13 = (bf16[8,512]{1,0:T(8,128)(2,1)S(1)}, bf16[8,512]{1,0:T(8,128)(2,1)S(1)}, u32[]{:S(2)}, u32[]{:S(2)}) collective-permute-start(bf16[8,512]{1,0:T(8,128)(2,1)S(1)} %collective-permute-done.11), channel_id=1, source_target_pairs={{0,30},{2,0},{4,2},{6,4},{8,6},{10,8},{12,10},{14,12},{16,14},{18,... | collective-permute-start | bytes 24584 | tf_op jit(solution)/shard_map/ppermute | solution.py:24
  84.9 7.2 %collective-permute-start.14 = (bf16[8,512]{1,0:T(8,128)(2,1)S(1)}, bf16[8,512]{1,0:T(8,128)(2,1)S(1)}, u32[]{:S(2)}, u32[]{:S(2)}) collective-permute-start(bf16[8,512]{1,0:T(8,128)(2,1)S(1)} %collective-permute-done.12), channel_id=1, source_target_pairs={{0,2},{2,4},{4,6},{6,8},{8,10},{10,12},{12,14},{14,16},{16,18},{18... | collective-permute-start | bytes 24584 | tf_op jit(solution)/shard_map/ppermute | solution.py:19
  84.9 7.2 %collective-permute-start.15 = (bf16[8,512]{1,0:T(8,128)(2,1)S(1)}, bf16[8,512]{1,0:T(8,128)(2,1)S(1)}, u32[]{:S(2)}, u32[]{:S(2)}) collective-permute-start(bf16[8,512]{1,0:T(8,128)(2,1)S(1)} %collective-permute-done.13), channel_id=1, source_target_pairs={{0,30},{2,0},{4,2},{6,4},{8,6},{10,8},{12,10},{14,12},{16,14},{18,... | collective-permute-start | bytes 24584 | tf_op jit(solution)/shard_map/ppermute | solution.py:24
  92.1 7.2 %collective-permute-start.16 = (bf16[8,512]{1,0:T(8,128)(2,1)S(1)}, bf16[8,512]{1,0:T(8,128)(2,1)S(1)}, u32[]{:S(2)}, u32[]{:S(2)}) collective-permute-start(bf16[8,512]{1,0:T(8,128)(2,1)S(1)} %collective-permute-done.14), channel_id=1, source_target_pairs={{0,2},{2,4},{4,6},{6,8},{8,10},{10,12},{12,14},{14,16},{16,18},{18... | collective-permute-start | bytes 24584 | tf_op jit(solution)/shard_map/ppermute | solution.py:19
  99.9 16.3 %copy-start.22 = (f32[256]{0:T(256)S(1)}, f32[256]{0:T(256)}, u32[]{:S(2)}) copy-start(f32[256]{0:T(256)} %param.22) | copy-start | bytes 3076
  121.1 1.3 copy-start.3
  122.4 8.5 %copy-start.20 = (s32[32]{0:T(128)S(1)}, s32[32]{0:T(128)}, u32[]{:S(2)}) copy-start(s32[32]{0:T(128)} %param.31) | copy-start | bytes 388
  131.0 14.4 %copy-start.10 = (bf16[512,256]{1,0:T(8,128)(2,1)S(1)}, bf16[512,256]{1,0:T(8,128)(2,1)}, u32[]{:S(2)}) copy-start(bf16[512,256]{1,0:T(8,128)(2,1)} %param.25) | copy-start | bytes 786436
  131.0 14.4 %copy-start.21 = (f32[256]{0:T(256)S(1)}, f32[256]{0:T(256)}, u32[]{:S(2)}) copy-start(f32[256]{0:T(256)} %param.26) | copy-start | bytes 3076
  138.7 9.5 %copy-start.24 = (s32[3]{0:T(128)S(1)}, s32[3]{0:T(128)}, u32[]{:S(2)}) copy-start(s32[3]{0:T(128)} %constant.170.clone.1) | copy-start | bytes 40
  145.4 21.8 %copy-start.5 = (bf16[512,512]{1,0:T(8,128)(2,1)S(1)}, bf16[512,512]{1,0:T(8,128)(2,1)}, u32[]{:S(2)}) copy-start(bf16[512,512]{1,0:T(8,128)(2,1)} %param.35) | copy-start | bytes 1572868
  145.4 21.8 %copy-start.19 = (f32[512]{0:T(512)S(1)}, f32[512]{0:T(512)}, u32[]{:S(2)}) copy-start(f32[512]{0:T(512)} %param.28) | copy-start | bytes 6148
  145.4 23.6 %copy-start.1 = (bf16[512,512]{1,0:T(8,128)(2,1)S(1)}, bf16[512,512]{1,0:T(8,128)(2,1)}, u32[]{:S(2)}) copy-start(bf16[512,512]{1,0:T(8,128)(2,1)} %param.19) | copy-start | bytes 1572868
  145.7 3.3 copy-start.13
  148.2 151.4 %reduce-scatter.3.cloned.1.call-start = ((), (), s32[]{:S(2)}) async-start(), calls=%async_computation.3 | async-start | bytes 139264 | tf_op jit(solution)/shard_map/reduce_scatter | solution.py:166
  164.1 4.9 %copy-start.2 = (f32[512,512]{1,0:T(8,128)S(1)}, f32[512,512]{1,0:T(8,128)}, u32[]{:S(2)}) copy-start(f32[512,512]{1,0:T(8,128)} %all-reduce.7.cloned.1.call-done) | copy-start | bytes 3145732
  164.1 6.2 %copy-start.14 = (f32[512,256]{1,0:T(8,128)S(1)}, f32[512,256]{1,0:T(8,128)}, u32[]{:S(2)}) copy-start(f32[512,256]{1,0:T(8,128)} %copy-done.13) | copy-start | bytes 1572868
  165.6 4.7 copy-start.25
  170.3 1.6 copy-start.11
  170.3 3.0 copy-start.12
  170.6 2.7 copy-start.7
  209.1 2.7 copy-start.23
  215.8 15.2 %collective-permute-start.17 = (bf16[128,256]{1,0:T(8,128)(2,1)S(1)}, bf16[128,256]{1,0:T(8,128)(2,1)S(1)}, u32[]{:S(2)}, u32[]{:S(2)}) collective-permute-start(bf16[128,256]{1,0:T(8,128)(2,1)S(1)} %bitcast.97), channel_id=1, source_target_pairs={{2,0},{4,2},{6,4},{8,6},{10,8},{12,10},{14,12},{16,14},{18,16},{20... | collective-permute-start | bytes 196616 | tf_op jit(solution)/shard_map/ppermute | solution.py:34
  221.4 9.7 %collective-permute-start.18 = (bf16[128,256]{1,0:T(8,128)(2,1)S(1)}, bf16[128,256]{1,0:T(8,128)(2,1)S(1)}, u32[]{:S(2)}, u32[]{:S(2)}) collective-permute-start(bf16[128,256]{1,0:T(8,128)(2,1)S(1)} %bitcast.98), channel_id=1, source_target_pairs={{30,0},{0,2},{2,4},{4,6},{6,8},{8,10},{10,12},{12,14},{14,16},{16,... | collective-permute-start | bytes 196616 | tf_op jit(solution)/shard_map/ppermute | solution.py:34
  222.3 130.8 %reduce-scatter.5.cloned.1.call-start = ((), (), s32[]{:S(2)}) async-start(), calls=%async_computation.4 | async-start | bytes 786432 | tf_op jit(solution)/shard_map/reduce_scatter | solution.py:179
  232.9 73.7 %copy-start.4 = (bf16[4096,256]{1,0:T(8,128)(2,1)S(1)}, bf16[4096,256]{1,0:T(8,128)(2,1)}, u32[]{:S(2)}) copy-start(bf16[4096,256]{1,0:T(8,128)(2,1)} %copy-done.3) | copy-start | bytes 6291460
  304.5 163.1 %all-reduce.9.cloned.1.call-start = ((), (), s32[]{:S(2)}) async-start(), calls=%async_computation.5 | async-start | bytes 6291456 | tf_op jit(solution)/shard_map/psum | solution.py:185
  311.1 1.2 copy-start.6
  467.6 4.3 copy-start.18
  467.6 5.4 %copy-start.17 = (f32[512,256]{0,1:T(8,128)S(1)}, f32[512,256]{0,1:T(8,128)}, u32[]{:S(2)}) copy-start(f32[512,256]{0,1:T(8,128)} %get-tuple-element.88) | copy-start | bytes 1572868
  467.6 6.4 %copy-start.16 = (f32[256,512]{1,0:T(8,128)S(1)}, f32[256,512]{1,0:T(8,128)}, u32[]{:S(2)}) copy-start(f32[256,512]{1,0:T(8,128)} %get-tuple-element.89) | copy-start | bytes 1572868
  468.8 6.1 %copy-start.15 = (f32[256,512]{1,0:T(8,128)S(1)}, f32[256,512]{1,0:T(8,128)}, u32[]{:S(2)}) copy-start(f32[256,512]{1,0:T(8,128)} %get-tuple-element.86) | copy-start | bytes 1572868
  (1 other events, 0.7 us)
Sparse Core Ops, SparseCore 0:
  148.3 15.7 all-reduce.6
  222.4 77.1 reduce-scatter.2
  304.6 4.2 reduce-scatter.4
  316.9 150.6 all-reduce.8
